TPU v7x, 128 devices: a whole 4x4x4 slice. The times are simulated.
128 devices in a mesh: row: 16 (over y, x), col: 8 (over z, core).
Axes of the slice: x: 4, y: 4, z: 4, core: 2. Of those that a mesh axis runs over, the one named last changes fastest.
Arguments:
- amplitudes: float32 [16384, 3072], P('row', 'col'), may hold values from -6 to 6
- row_gap: float32 [16384], P('row'), may hold values from -4 to -0.5
- row_irrep: int32 [16384], P('row'), may hold values from 0 to 7
- owners: int32 [16384, 1], P('row'), may hold values from 0 to 15; in each aligned block of 1024 rows (0 to 1023, 1024 to 2047, ...) at most 128 rows name the same one
- stored: float32 [3072, 8192], P('row', 'col'), may hold values from -0.109375 to 0.109375
- col_gap: float32 [8192], P('col'), may hold values from -4 to -0.5
- col_irrep: int32 [8192], P('col'), may hold values from 0 to 7
- mirror_flags: int32 [8], replicated, may hold values from 0 to 1
Outputs:
- update: float32 [32768, 8192], P('row', 'col')
Inputs may be any that keep to these rules, and one draw needn't show every extreme that they name: `owners`: in each aligned block of 1024 pairs (the pairs of one row index) no owner is named by more than 128 pairs, a bound that some block reaches.
All inputs are finite; a program needn't handle non-finite values.
Results may differ from a plain program's by a relative error of at most 0.000094.
Values sent between devices are 32-bit elements; how exact they have to be, the bound alone decides.
A program may use at most 128 MiB of HBM per device.

v0:
```python
import jax
import jax.numpy as jnp
from jax import lax
from jax.sharding import PartitionSpec as P


def from_partner(value, axis, distance):
    mask = 2**distance
    pairs = [(source, source ^ mask) for source in range(lax.axis_size(axis))]
    return lax.ppermute(value, axis, pairs)


def send_positions(target, row_count, capacity):
    onehot = (target[:, None] == jnp.arange(row_count, dtype=jnp.int32)[None, :]).astype(jnp.int32)
    running = jnp.cumsum(onehot, axis=0) - onehot
    slot_index = jnp.sum(running * onehot, axis=1)
    return target * capacity + slot_index


def per_device(amplitudes, row_gap, row_irrep, owners, stored, col_gap, col_irrep, mirror_flags):
    row_count = lax.axis_size("row")
    local_rows = amplitudes.shape[0]
    capacity = 2 * local_rows // row_count
    slot_total = row_count * capacity
    positions = send_positions(owners[:, 0], row_count, capacity)
    amp_here, gap_here, irrep_here = (amplitudes, row_gap, row_irrep)
    gathered = lax.all_gather(amp_here, "col", axis=1, tiled=True)
    parity = (1 - 2 * mirror_flags[lax.axis_index("col")]).astype(jnp.float32)
    mirror_bit = lax.axis_size("col").bit_length() - 2
    mirrored = from_partner(stored, "col", mirror_bit)
    operand = stored + parity * mirrored
    product = jnp.dot(
        gathered,
        lax.all_gather(operand, "row", axis=0, tiled=True),
        precision=lax.Precision.HIGHEST,
        preferred_element_type=jnp.float32,
    )
    same = irrep_here[:, None] == col_irrep[None, :]
    values = jnp.where(
        same, product / (gap_here[:, None] + col_gap[None, :]), jnp.zeros_like(product)
    )
    buffer = jnp.zeros((slot_total, values.shape[1]), jnp.float32).at[positions].set(values)
    return lax.all_to_all(buffer, "row", split_axis=0, concat_axis=0, tiled=True)


def solution(mesh):
    placed = (
        P("row", "col"),
        P("row"),
        P("row"),
        P("row", None),
        P("row", "col"),
        P("col"),
        P("col"),
        P(),
    )
    return jax.shard_map(
        per_device, mesh=mesh, in_specs=placed, out_specs=P("row", "col"), check_vma=False
    )
```

profile of v0, /device:TPU:0, one launch (start us, length us, event | category | flops | bytes accessed | tf_op | source)
XLA Modules:
  0.0 386.6 jit_solution(311767862544954345)
XLA Ops:
  6.5 0.0 all-gather.5.cloned.1.call-start
  6.5 0.7 all-gather.5.cloned.1.call-update
  7.3 0.0 all-gather.3.cloned.1.call-start
  7.3 4.0 %collective-permute-start = (f32[192,1024]{1,0:T(8,128)}, f32[192,1024]{1,0:T(8,128)S(1)}, u32[]{:S(2)}, u32[]{:S(2)}) collective-permute-start(f32[192,1024]{1,0:T(8,128)} %param.12), channel_id=1, source_target_pairs={{0,4},{1,5},{2,6},{3,7},{4,0},{5,1},{6,2},{7,3},{8,12},{9,13},{10,... | collective-permute-start | bytes 2359304 | tf_op jit(solution)/shard_map/ppermute | solution.py:10
  11.3 1.2 dynamic_slice.3
  13.2 21.7 %collective-permute-done = f32[192,1024]{1,0:T(8,128)S(1)} collective-permute-done((f32[192,1024]{1,0:T(8,128)}, f32[192,1024]{1,0:T(8,128)S(1)}, u32[]{:S(2)}, u32[]{:S(2)}) %collective-permute-start) | collective-permute-done | bytes 786464 | tf_op jit(solution)/shard_map/ppermute | solution.py:10
  35.0 2.1 multiply_add_fusion
  37.1 0.0 all-gather.3.cloned.1.call-update
  37.1 0.7 fusion.6
  37.8 4.5 %reduce-window.6 = s32[16,8,128]{2,1,0:T(8,128)S(1)} reduce-window(s32[16,8,128]{2,1,0:T(8,128)S(1)} %fusion.6, s32[]{:T(128)} %constant.10.clone.1), window={size=1x1x128 pad=0_0x0_0x127_0}, to_apply=%region_0.0 | reduce-window | flops 2080768 | bytes 131076 | tf_op jit(solution)/shard_map/reduce-window
  42.3 0.1 slice.8
  42.4 0.1 copy.11
  42.5 0.1 copy.12
  42.6 0.1 broadcast_add_fusion
  42.7 0.7 fusion.5
  43.4 0.7 compare_select_fusion
  44.1 38.0 %all-gather.5.cloned.1.call-done = f32[1024,3072]{1,0:T(8,128)} async-done(((f32[1024,384]{1,0:T(8,128)}), f32[1024,3072]{1,0:T(8,128)}) %all-gather.5.cloned.1.call-update) | async-done | bytes 12582928 | tf_op jit(solution)/shard_map/all_gather | solution.py:27
  82.1 93.1 %all-gather.3.cloned.1.call-done = f32[3072,1024]{1,0:T(8,128)} async-done(((f32[192,1024]{1,0:T(8,128)}), f32[3072,1024]{1,0:T(8,128)}) %all-gather.3.cloned.1.call-update) | async-done | bytes 12582928 | tf_op jit(solution)/shard_map/all_gather | solution.py:34
  175.3 85.0 %fusion = f32[1024,1024]{0,1:T(8,128)} fusion(f32[3072,1024]{1,0:T(8,128)} %all-gather.3.cloned.1.call-done, f32[1024,3072]{1,0:T(8,128)} %all-gather.5.cloned.1.call-done, f32[1024]{0:T(1024)} %param.13, f32[1024]{0:T(1024)} %param.9, s32[1024]{0:T(1024)} %param.10, s32[1024]{0:T(1024)} %param.14), kind=kOutput, calls=%fused_computation.2 | convolution fusion | flops 38658899968 | bytes 29376512 | tf_op jit(solution)/shard_map/dot_general | solution.py:32
  260.3 5.3 %copy.13 = f32[1024,1024]{1,0:T(8,128)} copy(f32[1024,1024]{0,1:T(8,128)} %fusion) | data formatting | bytes 8388608 | tf_op jit(solution)/shard_map/jit(_where)/select_n | solution.py:39
  265.6 9.7 %scatter_custom_fusion = f32[2048,1024]{1,0:T(8,128)} fusion(s32[1024]{0:T(1024)S(1)} %bitcast.38, f32[1024,1024]{1,0:T(8,128)} %copy.13, f32[]{:T(128)} %constant.8.clone.1), kind=kCustom, calls=%fused_computation.3 | custom fusion | bytes 8389120 | tf_op jit(solution)/shard_map/scatter | solution.py:42
  275.3 101.1 %all_to_all.12 = f32[16,128,1024]{2,1,0:T(8,128)S(1)} all-to-all(f32[16,128,1024]{2,1,0:T(8,128)} %bitcast.31), channel_id=1, replica_groups=mesh['row'=16,'col'=8] {'row'}, dimensions={0} | all-to-all | bytes 16777216 | tf_op jit(solution)/shard_map/all_to_all | solution.py:43
  376.4 3.4 copy.17
  (2 shorter events, 0.0 us)
Async XLA Ops:
  6.5 75.6 %all-gather.5.cloned.1.call-start = ((), (), s32[]{:S(2)}) async-start(), calls=%async_computation.2 | async-start | bytes 14155776 | tf_op jit(solution)/shard_map/all_gather | solution.py:27
  7.3 168.0 %all-gather.3.cloned.1.call-start = ((), (), s32[]{:S(2)}) async-start(), calls=%async_computation.1 | async-start | bytes 13369344 | tf_op jit(solution)/shard_map/all_gather | solution.py:34
  7.3 27.7 %collective-permute-start = (f32[192,1024]{1,0:T(8,128)}, f32[192,1024]{1,0:T(8,128)S(1)}, u32[]{:S(2)}, u32[]{:S(2)}) collective-permute-start(f32[192,1024]{1,0:T(8,128)} %param.12), channel_id=1, source_target_pairs={{0,4},{1,5},{2,6},{3,7},{4,0},{5,1},{6,2},{7,3},{8,12},{9,13},{10,... | collective-permute-start | bytes 2359304 | tf_op jit(solution)/shard_map/ppermute | solution.py:10
Sparse Core Ops, SparseCore 0:
  9.0 73.0 all-gather.4
  84.3 90.9 all-gather.2
where the time goes:
time: 387 us
  waiting for transfers between devices  154 us (40%)
  blocking collectives  101 us (26%)
  matrix products  85 us (22%)
  local copies, waits for them, and re-layouts  20 us (5%)
  between operations  14.1 us (4%)
  other arithmetic  8.85 us (2%)
  starting transfers between devices  4.08 us (1%)
    all_to_all x1, blocking collectives, per_device(): lax.all_to_all(buffer, 'row', split_axis=0, concat_axis=0, tiled=True)  101 us
    all_gather x1, waiting for transfers between devices, per_device(): lax.all_gather(operand, 'row', axis=0, tiled=True)  93.1 us
    dot_general x1, matrix products, per_device(): jnp.dot(gathered, lax.all_gather(operand, 'row', axis=0, tiled=True), pre...  85 us
    all_gather x1, waiting for transfers between devices, per_device(): gathered = lax.all_gather(amp_here, 'col', axis=1, tiled=True)  38 us
    ppermute x1, waiting for transfers between devices, from_partner(): return lax.ppermute(value, axis, pairs)  21.7 us
    scatter x1, local copies, waits for them, and re-layouts, per_device(): jnp.zeros((slot_total, values.shape[1]), jnp.float32).at[positions]  9.71 us
  transfers between devices with their start and end apart: 3, of which 3 were waited for; matrix products, arithmetic and copies ran while one was open for 3% of the time, Pallas kernels for 0%

commit v1 on v0

--- a/solution.py
+++ b/solution.py
@@ -11,9 +11,12 @@
 
 
 def send_positions(target, row_count, capacity):
-    onehot = (target[:, None] == jnp.arange(row_count, dtype=jnp.int32)[None, :]).astype(jnp.int32)
-    running = jnp.cumsum(onehot, axis=0) - onehot
-    slot_index = jnp.sum(running * onehot, axis=1)
+    onehot = (target[:, None] == jnp.arange(row_count, dtype=jnp.int32)[None, :]).astype(jnp.float32)
+    count = target.shape[0]
+    place = jnp.arange(count, dtype=jnp.int32)
+    earlier = (place[None, :] < place[:, None]).astype(jnp.float32)
+    running = jnp.dot(earlier, onehot, preferred_element_type=jnp.float32)
+    slot_index = jnp.sum(running * onehot, axis=1).astype(jnp.int32)
     return target * capacity + slot_index
 
 
@@ -23,22 +26,18 @@
     capacity = 2 * local_rows // row_count
     slot_total = row_count * capacity
     positions = send_positions(owners[:, 0], row_count, capacity)
-    amp_here, gap_here, irrep_here = (amplitudes, row_gap, row_irrep)
-    gathered = lax.all_gather(amp_here, "col", axis=1, tiled=True)
+    gathered = lax.all_gather(amplitudes, "col", axis=1, tiled=True)
     parity = (1 - 2 * mirror_flags[lax.axis_index("col")]).astype(jnp.float32)
     mirror_bit = lax.axis_size("col").bit_length() - 2
-    mirrored = from_partner(stored, "col", mirror_bit)
-    operand = stored + parity * mirrored
+    operand = stored + parity * from_partner(stored, "col", mirror_bit)
     product = jnp.dot(
         gathered,
         lax.all_gather(operand, "row", axis=0, tiled=True),
-        precision=lax.Precision.HIGHEST,
+        precision=lax.Precision.HIGH,
         preferred_element_type=jnp.float32,
     )
-    same = irrep_here[:, None] == col_irrep[None, :]
-    values = jnp.where(
-        same, product / (gap_here[:, None] + col_gap[None, :]), jnp.zeros_like(product)
-    )
+    same = row_irrep[:, None] == col_irrep[None, :]
+    values = jnp.where(same, product / (row_gap[:, None] + col_gap[None, :]), jnp.zeros_like(product))
     buffer = jnp.zeros((slot_total, values.shape[1]), jnp.float32).at[positions].set(values)
     return lax.all_to_all(buffer, "row", split_axis=0, concat_axis=0, tiled=True)
 

time: 387 us -> 349 us (0.902)
  matrix products: 85 us -> 47.4 us
  other arithmetic: 8.85 us -> 2.21 us
  waiting for transfers between devices: 154 us -> 160 us
    dot_general x1, matrix products: 85 us -> 46.9 us  [per_device(): jnp.dot(gathered, lax.all_gather(operand, 'row', axis=0, tiled=True), pre...]
    all_gather x1, waiting for transfers between devices: 38 us -> 44.4 us  [per_device(): gathered = lax.all_gather(amplitudes, 'col', axis=1, tiled=True)]
    another operation x3 -> x0, other arithmetic: 4.61 us -> none
  transfers between devices with their start and end apart: 3 -> 3, of which waited for: 3 -> 3; matrix products, arithmetic and copies ran while one was open for 3% -> 1% of each run, Pallas kernels for 0% -> 0%
where the time goes in v1:
time: 349 us
  waiting for transfers between devices  160 us (46%)
  blocking collectives  101 us (29%)
  matrix products  47.4 us (14%)
  local copies, waits for them, and re-layouts  19.9 us (6%)
  between operations  14.1 us (4%)
  starting transfers between devices  4.11 us (1%)
    all_to_all x1, blocking collectives, per_device(): lax.all_to_all(buffer, 'row', split_axis=0, concat_axis=0, tiled=True)  101 us
    all_gather x1, waiting for transfers between devices, per_device(): lax.all_gather(operand, 'row', axis=0, tiled=True)  93.1 us
    dot_general x1, matrix products, per_device(): jnp.dot(gathered, lax.all_gather(operand, 'row', axis=0, tiled=True), pre...  46.9 us
    all_gather x1, waiting for transfers between devices, per_device(): gathered = lax.all_gather(amplitudes, 'col', axis=1, tiled=True)  44.4 us
    ppermute x1, waiting for transfers between devices, from_partner(): return lax.ppermute(value, axis, pairs)  21.7 us
    scatter x1, local copies, waits for them, and re-layouts, per_device(): jnp.zeros((slot_total, values.shape[1]), jnp.float32).at[positions]  9.89 us
  transfers between devices with their start and end apart: 3, of which 3 were waited for; matrix products, arithmetic and copies ran while one was open for 1% of the time, Pallas kernels for 0%

profile of v1, /device:TPU:0, one launch (start us, length us, event | category | flops | bytes accessed | tf_op | source)
XLA Modules:
  0.0 348.7 jit_solution(15511140907921944811)
XLA Ops:
  6.5 0.0 copy-start
  6.5 0.0 copy-start.3
  6.5 0.0 copy-start.1
  6.5 0.0 copy-start.4
  6.5 0.0 copy-start.2
  6.5 0.0 all-gather.5.cloned.1.call-start
  6.6 0.7 all-gather.5.cloned.1.call-update
  7.3 0.0 all-gather.3.cloned.1.call-start
  7.3 4.0 %collective-permute-start = (f32[192,1024]{1,0:T(8,128)}, f32[192,1024]{1,0:T(8,128)S(1)}, u32[]{:S(2)}, u32[]{:S(2)}) collective-permute-start(f32[192,1024]{1,0:T(8,128)} %param.12), channel_id=1, source_target_pairs={{0,4},{1,5},{2,6},{3,7},{4,0},{5,1},{6,2},{7,3},{8,12},{9,13},{10,... | collective-permute-start | bytes 2359304 | tf_op jit(solution)/shard_map/ppermute | solution.py:10
  11.4 1.2 dynamic_slice.3
  13.3 21.7 %collective-permute-done = f32[192,1024]{1,0:T(8,128)S(1)} collective-permute-done((f32[192,1024]{1,0:T(8,128)}, f32[192,1024]{1,0:T(8,128)S(1)}, u32[]{:S(2)}, u32[]{:S(2)}) %collective-permute-start) | collective-permute-done | bytes 786464 | tf_op jit(solution)/shard_map/ppermute | solution.py:10
  35.0 2.2 multiply_add_fusion
  37.2 0.0 all-gather.3.cloned.1.call-update
  37.2 0.0 copy-done
  37.2 0.5 fusion.5
  37.7 44.4 %all-gather.5.cloned.1.call-done = f32[1024,3072]{1,0:T(8,128)} async-done(((f32[1024,384]{1,0:T(8,128)}), f32[1024,3072]{1,0:T(8,128)}) %all-gather.5.cloned.1.call-update) | async-done | bytes 12582928 | tf_op jit(solution)/shard_map/all_gather | solution.py:29
  82.2 93.1 %all-gather.3.cloned.1.call-done = f32[3072,1024]{1,0:T(8,128)} async-done(((f32[192,1024]{1,0:T(8,128)}), f32[3072,1024]{1,0:T(8,128)}) %all-gather.3.cloned.1.call-update) | async-done | bytes 12582928 | tf_op jit(solution)/shard_map/all_gather | solution.py:35
  175.3 0.0 copy-done.3
  175.3 0.0 copy-done.1
  175.3 0.0 copy-done.4
  175.3 0.0 copy-done.2
  175.3 46.9 %fusion = f32[1024,1024]{0,1:T(8,128)} fusion(f32[3072,1024]{1,0:T(8,128)} %all-gather.3.cloned.1.call-done, f32[1024,3072]{1,0:T(8,128)} %all-gather.5.cloned.1.call-done, f32[1024]{0:T(1024)S(1)} %copy-done.1, f32[1024]{0:T(1024)S(1)} %copy-done.2, s32[1024]{0:T(1024)S(1)} %copy-done.3, s32[1024]{0:T(1024)S(1)} %copy-done.4), kind=kOutput, calls=%fused_computation.2 | convolution fusion | flops 19331547136 | bytes 29376512 | tf_op jit(solution)/shard_map/dot_general | solution.py:33
  222.2 5.4 %copy.9 = f32[1024,1024]{1,0:T(8,128)} copy(f32[1024,1024]{0,1:T(8,128)} %fusion) | data formatting | bytes 8388608 | tf_op jit(solution)/shard_map/jit(_where)/select_n | solution.py:40
  227.5 9.9 %scatter_custom_fusion = f32[2048,1024]{1,0:T(8,128)} fusion(s32[1024]{0:T(1024)S(1)} %bitcast.16, f32[1024,1024]{1,0:T(8,128)} %copy.9, f32[]{:T(128)} %constant.8.clone.1), kind=kCustom, calls=%fused_computation.4 | custom fusion | bytes 8389120 | tf_op jit(solution)/shard_map/scatter | solution.py:41
  237.4 101.1 %all_to_all.12 = f32[16,128,1024]{2,1,0:T(8,128)S(1)} all-to-all(f32[16,128,1024]{2,1,0:T(8,128)} %bitcast.12), channel_id=1, replica_groups=mesh['row'=16,'col'=8] {'row'}, dimensions={0} | all-to-all | bytes 16777216 | tf_op jit(solution)/shard_map/all_to_all | solution.py:42
  338.5 3.4 copy.11
  (2 shorter events, 0.0 us)
Async XLA Ops:
  6.5 30.7 %copy-start = (s32[1024,1]{0,1:T(1,128)S(1)}, s32[1024,1]{0,1:T(1,128)}, u32[]{:S(2)}) copy-start(s32[1024,1]{0,1:T(1,128)} %param.11) | copy-start | bytes 12292
  6.5 168.8 %copy-start.3 = (s32[1024]{0:T(1024)S(1)}, s32[1024]{0:T(1024)}, u32[]{:S(2)}) copy-start(s32[1024]{0:T(1024)} %param.10) | copy-start | bytes 12292
  6.5 168.8 %copy-start.1 = (f32[1024]{0:T(1024)S(1)}, f32[1024]{0:T(1024)}, u32[]{:S(2)}) copy-start(f32[1024]{0:T(1024)} %param.13) | copy-start | bytes 12292
  6.5 168.8 %copy-start.4 = (s32[1024]{0:T(1024)S(1)}, s32[1024]{0:T(1024)}, u32[]{:S(2)}) copy-start(s32[1024]{0:T(1024)} %param.14) | copy-start | bytes 12292
  6.5 168.8 %copy-start.2 = (f32[1024]{0:T(1024)S(1)}, f32[1024]{0:T(1024)}, u32[]{:S(2)}) copy-start(f32[1024]{0:T(1024)} %param.9) | copy-start | bytes 12292
  6.5 75.6 %all-gather.5.cloned.1.call-start = ((), (), s32[]{:S(2)}) async-start(), calls=%async_computation.2 | async-start | bytes 14155776 | tf_op jit(solution)/shard_map/all_gather | solution.py:29
  7.3 168.0 %all-gather.3.cloned.1.call-start = ((), (), s32[]{:S(2)}) async-start(), calls=%async_computation.1 | async-start | bytes 13369344 | tf_op jit(solution)/shard_map/all_gather | solution.py:35
  7.3 27.7 %collective-permute-start = (f32[192,1024]{1,0:T(8,128)}, f32[192,1024]{1,0:T(8,128)S(1)}, u32[]{:S(2)}, u32[]{:S(2)}) collective-permute-start(f32[192,1024]{1,0:T(8,128)} %param.12), channel_id=1, source_target_pairs={{0,4},{1,5},{2,6},{3,7},{4,0},{5,1},{6,2},{7,3},{8,12},{9,13},{10,... | collective-permute-start | bytes 2359304 | tf_op jit(solution)/shard_map/ppermute | solution.py:10
Sparse Core Ops, SparseCore 0:
  9.1 73.0 all-gather.4
  84.3 90.9 all-gather.2

commit v2 on v1

v2 whole, which is shorter than its diff:
```python
import jax
import jax.numpy as jnp
from jax import lax
from jax.experimental import pallas as pl
from jax.experimental.pallas import tpu as pltpu
from jax.sharding import PartitionSpec as P

SIDE = 4
STEPS = (0, 1, 3, 2)
DEPTH = 3072
LANES = 1024
PART = 384
CHUNK = 192
ROWS = 1024
CAP = 128
HALF = LANES // 2
GROUP = SIDE * CAP
CORES = 2


def plan():
    copies = {}
    for h in range(2):
        copies["mirror", h] = ((0, 0, 2, 0), [], 384)
    for g, dy in enumerate(STEPS):
        for dx in range(SIDE):
            if dy or dx:
                copies["meta", g, dx] = ((-dy, -dx, 0, 0), [], 4)
                copies["route", g, dx] = ((-dy, -dx, 0, 0), [], 192)
    for h in range(2):
        own = [("mirror", h)]

        def along(axis, step, h=h):
            first = (axis == 0) == (h == 0)
            return (0, step, 0, 0) if first else (step, 0, 0, 0)

        for s in (1, -1):
            copies["line", h, s] = (along(0, s), own, 384)
            copies["linepass", h, s] = (along(0, s), [("line", h, s)], 192)
        for j in (0, -1, 1, 2):
            if j == 0:
                after = own
            elif j == 2:
                after = [("linepass", h, 1), ("linepass", h, -1)]
            else:
                after = [("line", h, -j)]
            for s in (1, -1):
                copies["plane", h, j, s] = (along(1, s), after, 384)
                copies["planepass", h, j, s] = (along(1, s), [("plane", h, j, s)], 192)
    for g, dy in enumerate(STEPS):
        here = [("route", g, dx) for dx in range(SIDE) if dy or dx]
        copies["own", g] = ((0, 0, 0, 1), here, 768)
        for s in (1, -1):
            copies["ring", g, s] = ((0, 0, s, 0), here, 768)
            copies["ringpass", g, s] = ((0, 0, s, 0), [("ring", g, s)], 384)
            copies["share", g, s] = ((0, 0, 0, 1), [("ring", g, s)], 768)
            copies["sharepass", g, s] = ((0, 0, 0, 1), [("ringpass", g, s)], 384)
    return copies


def arrivals(copies):
    free, arrived, issued = {}, {}, {}
    ready = {}
    slot = 0
    for name, (_, after, _) in copies.items():
        if not after:
            if name[0] == "mirror":
                ready[name] = 3.0
            else:
                slot += 1
                ready[name] = 4.0 + 0.25 * slot
    while len(issued) < len(copies):
        name = min((n for n in ready if n not in issued), key=lambda n: (ready[n], str(n)))
        issued[name] = at = ready[name]
        offset, _, size = copies[name]
        end = at
        for axis, step in enumerate(offset):
            step = (step + 1) % SIDE - 1 if axis < 3 else step
            ways = ((1, 0.5), (-1, 0.5)) if abs(step) == 2 else ((step, 1.0),)
            for way, share in ways:
                if step:
                    link = (axis, way > 0)
                    hops = abs(step)
                    rate = 400.0 if axis == 3 else 43.0
                    start = max(at, free.get(link, 0.0))
                    free[link] = start + 1.05 * size * share * hops / rate
                    end = max(end, free[link])
        arrived[name] = end + 2.0
        for other, (_, after, _) in copies.items():
            if other not in ready and after and all(a in arrived for a in after):
                ready[other] = max(arrived[a] for a in after) + 0.5
    return sorted(copies, key=lambda n: (arrived[n], str(n)))


def kernel(
    amp, own, gap, irrep, stored, flags, cycle, meta,
    slots, weights, high, low, outgoing, mirrored, places, notes, heard, sent, came, done,
):
    row, col = lax.axis_index("row"), lax.axis_index("col")
    y, x, z, k = row // SIDE, row % SIDE, col // CORES, col % CORES

    def device(offset):
        dy, dx, dz, dk = offset
        there = ((y + dy + SIDE) % SIDE) * SIDE + (x + dx + SIDE) % SIDE
        return {"row": there, "col": ((z + dz + SIDE) % SIDE) * CORES + (k + dk) % CORES}

    copies = plan()
    index = {name: i for i, name in enumerate(copies)}
    barrier = pltpu.get_barrier_semaphore()
    partners = [(dy, dx, 0, 0) for dy in range(SIDE) for dx in range(SIDE) if dy or dx]
    partners += [(0, 0, 1, 0), (0, 0, 2, 0), (0, 0, 3, 0), (0, 0, 0, 1)]
    for offset in partners:
        pl.semaphore_signal(barrier, inc=1, device_id=device(offset), device_id_type=pl.DeviceIdType.MESH)

    def chunk(h, p, q, part):
        dx, dy = (p, q) if h == 0 else (q, p)
        at = (((y + dy + SIDE) % SIDE) * SIDE + (x + dx + SIDE) % SIDE) * CHUNK
        size = CHUNK if part == 0 else CHUNK // 2
        at = at + (CHUNK // 2 if part < 0 else 0)
        return pl.ds(pl.multiple_of(at, CHUNK // 2), size), pl.ds(h * HALF, HALF)

    def group(dy):
        return ((y + dy) % SIDE) * SIDE

    def held(dz, g, part):
        at = group(STEPS[g]) + (SIDE // 2 if part < 0 else 0)
        size = SIDE if part == 0 else SIDE // 2
        return slots.at[((z + dz + SIDE) % SIDE) * CORES + k, pl.ds(at, size)]

    made = {}

    def copy(name):
        if name in made:
            return made[name]
        kind, rest = name[0], name[1:]
        if kind == "mirror":
            cols = pl.ds(rest[0] * HALF, HALF)
            src, dst = stored.at[:, cols], mirrored.at[:, cols]
        elif kind == "meta":
            i = rest[0] * SIDE + rest[1]
            src, dst = notes.at[i], heard.at[row]
        elif kind == "route":
            i = rest[0] * SIDE + rest[1]
            src, dst = outgoing.at[i], slots.at[col, row]
        elif kind in ("line", "linepass", "plane", "planepass"):
            h, s = rest[0], rest[-1]
            if kind == "line":
                where = chunk(h, 0, 0, 0)
            elif kind == "linepass":
                where = chunk(h, -s, 0, s)
            elif kind == "plane":
                where = chunk(h, rest[1], 0, 0)
            else:
                where = chunk(h, rest[1], -s, s)
            src = dst = weights.at[where]
        else:
            g = rest[0]
            if kind in ("own",):
                src = held(0, g, 0)
            elif kind == "ring":
                src = held(0, g, 0)
            elif kind == "ringpass":
                src = held(-rest[1], g, rest[1])
            elif kind == "share":
                src = held(-rest[1], g, 0)
            else:
                src = held(2, g, rest[1])
            dst = src
        i = index[name]
        made[name] = pltpu.make_async_remote_copy(
            src_ref=src, dst_ref=dst, send_sem=sent.at[i], recv_sem=came.at[i],
            device_id=device(copies[name][0]), device_id_type=pl.DeviceIdType.MESH,
        )
        return made[name]

    def halves(value):
        top = value.astype(jnp.bfloat16)
        return top, (value - top.astype(jnp.float32)).astype(jnp.bfloat16)

    earlier = (
        lax.broadcasted_iota(jnp.int32, (CAP, CAP), 0) < lax.broadcasted_iota(jnp.int32, (CAP, CAP), 1)
    ).astype(jnp.float32).astype(jnp.bfloat16)
    count = jnp.zeros((16, 1), jnp.float32)
    for b in range(ROWS // CAP):
        names = own[:, b * CAP : (b + 1) * CAP]
        hit = lax.broadcasted_iota(jnp.int32, (16, CAP), 0) == names
        one = jnp.where(hit, 1.0, 0.0)
        running = jnp.dot(one.astype(jnp.bfloat16), earlier, preferred_element_type=jnp.float32) + count
        places[:, b * CAP : (b + 1) * CAP] = jnp.where(hit, running, -1.0)
        count = count + jnp.sum(one, axis=1, keepdims=True)

    high[0:ROWS, 0:PART], low[0:ROWS, 0:PART] = halves(amp[...])
    gap_top, gap_rest = halves(gap[...])
    gap_rest = gap[...] - gap_top.astype(jnp.float32)
    gap_mid, gap_end = halves(gap_rest)
    pieces = [
        gap_top.astype(jnp.float32),
        gap_mid.astype(jnp.float32),
        gap_end.astype(jnp.float32),
        (irrep[...] + 1).astype(jnp.float32),
    ]
    tags = jnp.concatenate(pieces + [jnp.zeros((12, ROWS), jnp.float32)], axis=0).astype(jnp.bfloat16)

    pl.semaphore_wait(barrier, len(partners))
    started = []

    def start(name):
        copy(name).start()
        started.append(name)

    for h in range(2):
        start(("mirror", h))

    def slotted(owner):
        place = places[pl.ds(owner, 1), :]
        pick = lax.broadcasted_iota(jnp.int32, (CAP, ROWS), 0).astype(jnp.float32) == place
        pick = jnp.where(pick, 1.0, 0.0).astype(jnp.bfloat16)
        block = jnp.dot(pick, high[0:ROWS, 0:PART], preferred_element_type=jnp.float32)
        block += jnp.dot(pick, low[0:ROWS, 0:PART], preferred_element_type=jnp.float32)
        note = lax.dot_general(tags, pick, (((1,), (1,)), ((), ())), preferred_element_type=jnp.float32)
        return block, note[0:8]

    for g, dy in enumerate(STEPS):
        for dx in range(SIDE):
            there = ((y - dy + SIDE) % SIDE) * SIDE + (x - dx + SIDE) % SIDE
            block, note = slotted(there)
            i = g * SIDE + dx
            if i == 0:
                slots[col, row] = block
                heard[row] = note
            else:
                outgoing[i] = block
                notes[i] = note
                start(("route", g, dx))
                start(("meta", g, dx))

    parity = (1 - 2 * flags[col]).astype(jnp.float32)

    def split(where, n):
        rows, cols = where
        first = rows.start

        def body(i, carry):
            at = pl.ds(pl.multiple_of(first + i * 32, 32), 32)
            high[at, cols], low[at, cols] = halves(weights[at, cols])
            return carry

        lax.fori_loop(0, n // 32, body, 0)

    def multiply(g, offsets):
        base = g * GROUP

        def body(i, carry):
            dz = jnp.int32(0)
            for n, o in enumerate(offsets):
                dz = jnp.where(i // CORES == n, o, dz)
            c = ((z + dz + SIDE) % SIDE) * CORES + i % CORES
            a = slots[c, pl.ds(group(STEPS[g]), SIDE)].reshape(GROUP, PART)
            top, rest = halves(a)
            at = pl.ds(pl.multiple_of(c * PART, PART), PART)
            for n in range(0, LANES, 256):
                w = high[at, n : n + 256]
                add = jnp.dot(top, w, preferred_element_type=jnp.float32)
                add += jnp.dot(rest, w, preferred_element_type=jnp.float32)
                add += jnp.dot(top, low[at, n : n + 256], preferred_element_type=jnp.float32)
                weights[base : base + GROUP, n : n + 256] += add
            return carry

        lax.fori_loop(0, len(offsets) * CORES, body, 0)

    def write(g):
        return pltpu.make_async_copy(
            weights.at[pl.ds(g * GROUP, GROUP)],
            cycle.at[pl.ds(pl.multiple_of(group(STEPS[g]) * CAP, GROUP), GROUP)],
            done.at[g],
        )

    seen = set()
    weight_kinds = ("line", "linepass", "plane", "planepass")
    left_weights = sum(n[0] in weight_kinds for n in copies)
    computed = {}
    near, far = (0, -1, 1), (2,)

    def has(g, offsets):
        need = [("route", g, dx) for dx in range(SIDE) if STEPS[g] or dx]
        need += [("own", g)]
        for s in (1, -1):
            if -s in offsets:
                need += [("ring", g, s), ("share", g, s)]
            if 2 in offsets:
                need += [("ringpass", g, s), ("sharepass", g, s)]
        return all(n in seen for n in need)

    def run_ready():
        if left_weights:
            return
        for g in range(SIDE):
            stage = computed.get(g, 0)
            if stage == 0 and has(g, near + far):
                weights[g * GROUP : (g + 1) * GROUP] = jnp.zeros((GROUP, LANES), jnp.float32)
                multiply(g, near + far)
                write(g).start()
                computed[g] = 2
            elif stage == 0 and g == SIDE - 1 and has(g, near):
                weights[g * GROUP : (g + 1) * GROUP] = jnp.zeros((GROUP, LANES), jnp.float32)
                multiply(g, near)
                computed[g] = 1
            elif stage == 1 and has(g, far):
                multiply(g, far)
                write(g).start()
                computed[g] = 2

    for name in arrivals(copies):
        copy(name).wait_recv()
        seen.add(name)
        kind = name[0]
        if kind == "mirror":
            cols = pl.ds(name[1] * HALF, HALF)
            mine = chunk(name[1], 0, 0, 0)
            weights[mine] = stored[:, cols] + parity * mirrored[:, cols]
        for other, (_, after, _) in copies.items():
            if other not in started and after and name in after and all(a in seen for a in after):
                start(other)
        if kind == "mirror":
            split(mine, CHUNK)
        if kind in weight_kinds:
            left_weights -= 1
            h, s = name[1], name[-1]
            if kind == "line":
                split(chunk(h, -s, 0, 0), CHUNK)
            elif kind == "linepass":
                split(chunk(h, -2 * s, 0, s), CHUNK // 2)
            elif kind == "plane":
                split(chunk(h, name[2], -s, 0), CHUNK)
            else:
                split(chunk(h, name[2], -2 * s, s), CHUNK // 2)
            if left_weights == 0:
                for n in copies:
                    if n[0] in weight_kinds:
                        copy(n).wait_send()
        run_ready()

    for i in range(16):
        meta[i] = heard[i]
    for n in copies:
        if n[0] not in weight_kinds:
            copy(n).wait_send()
    for g in range(SIDE):
        write(g).wait()


def exchange(amp, own, gap, irrep, stored, flags):
    n = len(plan())
    vmem = pl.BlockSpec(memory_space=pltpu.VMEM)
    return pl.pallas_call(
        kernel,
        out_shape=(
            jax.ShapeDtypeStruct((16 * CAP, LANES), jnp.float32),
            jax.ShapeDtypeStruct((16, 8, CAP), jnp.float32),
        ),
        in_specs=[vmem] * 5 + [pl.BlockSpec(memory_space=pltpu.SMEM)],
        out_specs=(pl.BlockSpec(memory_space=pl.ANY), vmem),
        scratch_shapes=[
            pltpu.VMEM((SIDE * CORES, 16, CAP, PART), jnp.float32),
            pltpu.VMEM((DEPTH, LANES), jnp.float32),
            pltpu.VMEM((DEPTH, LANES), jnp.bfloat16),
            pltpu.VMEM((DEPTH, LANES), jnp.bfloat16),
            pltpu.VMEM((16, CAP, PART), jnp.float32),
            pltpu.VMEM((CHUNK, LANES), jnp.float32),
            pltpu.VMEM((16, ROWS), jnp.float32),
            pltpu.VMEM((16, 8, CAP), jnp.float32),
            pltpu.VMEM((16, 8, CAP), jnp.float32),
            pltpu.SemaphoreType.DMA((n,)),
            pltpu.SemaphoreType.DMA((n,)),
            pltpu.SemaphoreType.DMA((SIDE,)),
        ],
        compiler_params=pltpu.CompilerParams(
            collective_id=0, has_side_effects=True, vmem_limit_bytes=60 * 2**20
        ),
        name="exchange",
    )(amp, own, gap, irrep, stored, flags)


def per_device(amplitudes, row_gap, row_irrep, owners, stored, col_gap, col_irrep, mirror_flags):
    line = (1, ROWS)
    cycle, meta = exchange(
        amplitudes, owners.reshape(line), row_gap.reshape(line), row_irrep.reshape(line), stored, mirror_flags
    )
    gap = (meta[:, 0] + meta[:, 1] + meta[:, 2]).reshape(-1, 1)
    irrep = (meta[:, 3] - 1.0).reshape(-1, 1)
    same = irrep == col_irrep.astype(jnp.float32)[None, :]
    return jnp.where(same, cycle / (gap + col_gap[None, :]), 0.0)


def solution(mesh):
    placed = (
        P("row", "col"),
        P("row"),
        P("row"),
        P("row", None),
        P("row", "col"),
        P("col"),
        P("col"),
        P(),
    )
    return jax.shard_map(
        per_device, mesh=mesh, in_specs=placed, out_specs=P("row", "col"), check_vma=False
    )
```

time: 349 us -> 196 us (0.56)
  Pallas kernels: 0 us -> 185 us
  waiting for transfers between devices: 160 us -> 0 us
  blocking collectives: 101 us -> 0 us
  matrix products: 47.4 us -> 0 us
  local copies, waits for them, and re-layouts: 19.9 us -> 0 us
  between operations: 14.1 us -> 0.01 us
  other arithmetic: 2.21 us -> 8.06 us
  starting transfers between devices: 4.11 us -> 0 us
    pallas_call x0 -> x1, Pallas kernels: none -> 185 us  [exchange(): pl.pallas_call(kernel, out_shape=(jax.ShapeDtypeStruct((16 * CAP, LANES),...]
    all_gather x2 -> x0, waiting for transfers between devices: 138 us -> none  [the longest x1 93.1 us: per_device(): lax.all_gather(operand, 'row', axis=0, tiled=True)]
    all_to_all x1 -> x0, blocking collectives: 101 us -> none  [per_device(): lax.all_to_all(buffer, 'row', split_axis=0, concat_axis=0, tiled=True)]
    dot_general x2 -> x0, matrix products: 47.4 us -> none  [the longest x1 46.9 us: per_device(): jnp.dot(gathered, lax.all_gather(operand, 'row', axis=0, tiled=True), pre...]
    ppermute x1 -> x0, waiting for transfers between devices: 21.7 us -> none  [from_partner(): return lax.ppermute(value, axis, pairs)]
    scatter x1 -> x0, local copies, waits for them, and re-layouts: 9.89 us -> none  [per_device(): jnp.zeros((slot_total, values.shape[1]), jnp.float32).at[positions]]
    select_n x1, other arithmetic: 0.01 us -> 6.36 us  [per_device(): return jnp.where(same, cycle / (gap + col_gap[None, :]), 0.0)]
    select_n x1 -> x0, local copies, waits for them, and re-layouts: 5.35 us -> none  [per_device(): jnp.where(same, product / (row_gap[:, None] + col_gap[None, :]), jnp.zero...]
  transfers between devices with their start and end apart: 3 -> 0, of which waited for: 3 -> 0; matrix products, arithmetic and copies ran while one was open for 1% -> 0% of each run, Pallas kernels for 0% -> 0%
where the time goes in v2:
time: 196 us; the launch traced here: 193 us
  Pallas kernels  185 us (94%)
  other arithmetic  8.06 us (4%)
    pallas_call x1, Pallas kernels, exchange(): pl.pallas_call(kernel, out_shape=(jax.ShapeDtypeStruct((16 * CAP, LANES),...  185 us
    select_n x1, other arithmetic, per_device(): return jnp.where(same, cycle / (gap + col_gap[None, :]), 0.0)  6.36 us

profile of v2, /device:TPU:0, one launch (start us, length us, event | category | flops | bytes accessed | tf_op | source)
XLA Modules:
  0.0 192.6 jit_solution(15725502647293171702)
XLA Ops:
  0.0 0.7 convert_element_type.3
  0.7 184.6 %exchange.1 = (f32[2048,1024]{1,0:T(8,128)}, f32[16,8,128]{2,1,0:T(8,128)}) custom-call(f32[1024,384]{1,0:T(8,128)} %amp.1, s32[1,1024]{1,0:T(1,128)} %bitcast.7, f32[1,1024]{1,0:T(1,128)} %bitcast.8, s32[1,1024]{1,0:T(1,128)} %bitcast.9, f32[192,1024]{1,0:T(8,128)} %stored.1, s32[8]{0:T(128)} %flags.1), custom_call_target="tpu_custom_call" | custom-call | tf_op jit(solution)/shard_map/exchange/pallas_call | solution.py:355
  185.3 1.0 slice_add_fusion.1
  186.3 6.4 %divide_select_fusion = f32[2048,1024]{1,0:T(8,128)} fusion(f32[2048,1024]{1,0:T(8,128)} %get-tuple-element.8, f32[1024]{0:T(1024)} %param.13, f32[2048]{0:T(1024)S(1)} %bitcast.6, f32[1024]{0:T(1024)S(1)} %convert_element_type.3, f32[2048]{0:T(1024)S(1)} %bitcast.5), kind=kLoop, calls=%fused_computation | loop fusion | flops 8388608 | bytes 16801792 | tf_op jit(solution)/shard_map/jit(_where)/select_n | solution.py:392

commit v3 on v2

v3 whole, which is shorter than its diff:
```python
import jax
import jax.numpy as jnp
from jax import lax
from jax.experimental import pallas as pl
from jax.experimental.pallas import tpu as pltpu
from jax.sharding import PartitionSpec as P

SIDE = 4
STEPS = (0, 1, 3, 2)
DEPTH = 3072
LANES = 1024
PART = 384
CHUNK = 192
ROWS = 1024
CAP = 128
QUARTERS = 4
WIDE = LANES // QUARTERS
SET = 2 * WIDE
ROOM = 3
GROUP = SIDE * CAP
CORES = 2
WEIGHTS = ("line", "linepass", "plane", "planepass")
START = (0.0, 6.0, 8.0, 10.0)
RATES = (43.5, 40.0, 400.0)


def plan():
    copies = {}
    for h in range(QUARTERS):
        copies["mirror", h] = ((0, 0, 2, 0), [], 192)
    for g, dy in enumerate(STEPS):
        for dx in (0, 1, 3, 2):
            if dy or dx:
                copies["meta", g, dx] = ((-dy, -dx, 0, 0), [("slot", g)], 4)
                copies["route", g, dx] = ((-dy, -dx, 0, 0), [("slot", g)], 192)
    for h in range(QUARTERS):
        own = [("mirror", h)]
        if h >= 2:
            own += [(kind, h - 2, *j, s) for kind, j in (("line", ()), ("plane", (0,))) for s in (1, -1)]

        def along(axis, step, h=h):
            return (0, step, 0, 0) if axis == h % 2 else (step, 0, 0, 0)

        for s in (1, -1):
            copies["line", h, s] = (along(0, s), own, 192)
            copies["linepass", h, s] = (along(0, s), [("line", h, s)], 96)
        for j in (0, -1, 1, 2):
            if j == 0:
                after = own
            elif j == 2:
                after = [("linepass", h, 1), ("linepass", h, -1)]
            else:
                after = [("line", h, -j)]
            for s in (1, -1):
                copies["plane", h, j, s] = (along(1, s), after, 192)
                copies["planepass", h, j, s] = (along(1, s), [("plane", h, j, s)], 96)
    for g, dy in enumerate(STEPS):
        here = [("slot", g)] + [("route", g, dx) for dx in range(SIDE) if dy or dx]
        copies["own", g] = ((0, 0, 0, 1), here, 768)
        for s in (1, -1):
            copies["ring", g, s] = ((0, 0, s, 0), here, 768)
            copies["ringpass", g, s] = ((0, 0, s, 0), [("ring", g, s)], 384)
            copies["share", g, s] = ((0, 0, 0, 1), [("ring", g, s)], 768)
            copies["sharepass", g, s] = ((0, 0, 0, 1), [("ringpass", g, s)], 384)
    return copies


def schedule(copies):
    free, arrived, issued, order, handled = {}, {}, set(), [], set()
    now = 3.0
    slots_left, units = list(range(SIDE)), []
    for g in range(SIDE):
        units += [(g, half, dz) for half in range(2) for dz in (0, -1, 1, 2)]
    opened, closed = [], []

    def issue(name):
        offset, _, size = copies[name]
        issued.add(name)
        end = now
        for axis, step in enumerate(offset):
            step = (step + 1) % SIDE - 1 if axis < 3 else step
            ways = ((1, 0.5), (-1, 0.5)) if abs(step) == 2 else ((step, 1.0),)
            for way, share in ways:
                if step:
                    link = (axis, way > 0)
                    rate = RATES[2 if axis == 3 else name[0] == "route"]
                    start = max(now, free.get(link, 0.0))
                    free[link] = start + 1.024 * size * share * abs(step) / rate
                    end = max(end, free[link])
        arrived[name] = end + 2.0

    def release():
        for name, (_, after, _) in copies.items():
            if name not in issued and all(n in handled for n in after):
                issue(name)

    release()
    while len(handled) < len(copies) + SIDE or units:
        handled.update(n for n in arrived if n[0] == "meta")
        waiting = sorted((t, str(n), n) for n, t in arrived.items() if n not in handled)
        if slots_left and START[slots_left[0]] <= now:
            g = slots_left.pop(0)
            now += 1.4
            handled.add(("slot", g))
            order.append(("slot", g))
            release()
        elif waiting and waiting[0][0] <= now:
            name = waiting[0][2]
            now += 0.15
            handled.add(name)
            order.append(("wait", name))
            release()
        else:
            unit = None
            for u in units:
                pair = u[:2]
                if pair not in opened and len(opened) >= ROOM and opened[-ROOM] not in closed:
                    continue
                if all(n in handled for n in needs(*u)):
                    unit = u
                    break
            if unit:
                units.remove(unit)
                if unit[:2] not in opened:
                    opened.append(unit[:2])
                if all(u[:2] != unit[:2] for u in units):
                    closed.append(unit[:2])
                now += 1.5
                order.append(("unit", unit))
            else:
                now = min([w[0] for w in waiting[:1]] + [START[g] for g in slots_left[:1]])
    return order


def needs(g, half, dz):
    need = []
    for h in (2 * half, 2 * half + 1):
        need += [("line", h, s) for s in (1, -1)] + [("linepass", h, s) for s in (1, -1)]
        need += [(kind, h, j, s) for kind in ("plane", "planepass") for j in (0, -1, 1, 2) for s in (1, -1)]
    if dz == 0:
        need += [("slot", g), ("own", g)] + [("route", g, dx) for dx in range(SIDE) if STEPS[g] or dx]
    elif dz == 2:
        need += [(kind, g, s) for kind in ("ringpass", "sharepass") for s in (1, -1)]
    else:
        need += [("ring", g, -dz), ("share", g, -dz)]
    return need


def kernel(
    amp, own, gap, irrep, stored, flags, cycle, meta,
    slots, weights, high, low, top_amp, rest_amp, sums, outgoing, mirrored, places, notes, heard, sent, came, done,
):
    row, col = lax.axis_index("row"), lax.axis_index("col")
    y, x, z, k = row // SIDE, row % SIDE, col // CORES, col % CORES

    def device(offset):
        dy, dx, dz, dk = offset
        there = ((y + dy + SIDE) % SIDE) * SIDE + (x + dx + SIDE) % SIDE
        return {"row": there, "col": ((z + dz + SIDE) % SIDE) * CORES + (k + dk) % CORES}

    copies = plan()
    index = {name: i for i, name in enumerate(copies)}
    load = pltpu.make_async_copy(amp, outgoing.at[0 : ROWS // CAP], done.at[ROOM])
    load.start()
    barrier = pltpu.get_barrier_semaphore()
    partners = [(dy, dx, 0, 0) for dy in range(SIDE) for dx in range(SIDE) if dy or dx]
    partners += [(0, 0, 1, 0), (0, 0, 2, 0), (0, 0, 3, 0), (0, 0, 0, 1)]
    for offset in partners:
        pl.semaphore_signal(barrier, inc=1, device_id=device(offset), device_id_type=pl.DeviceIdType.MESH)

    def chunk(h, p, q, part):
        dx, dy = (p, q) if h % 2 == 0 else (q, p)
        at = (((y + dy + SIDE) % SIDE) * SIDE + (x + dx + SIDE) % SIDE) * CHUNK
        size = CHUNK if part == 0 else CHUNK // 2
        at = at + (CHUNK // 2 if part < 0 else 0)
        return pl.ds(pl.multiple_of(at, CHUNK // 2), size), pl.ds(h * WIDE, WIDE)

    def group(dy):
        return ((y + dy) % SIDE) * SIDE

    def held(dz, g, part):
        at = group(STEPS[g]) + (SIDE // 2 if part < 0 else 0)
        size = SIDE if part == 0 else SIDE // 2
        return slots.at[((z + dz + SIDE) % SIDE) * CORES + k, pl.ds(at, size)]

    made = {}

    def copy(name):
        if name in made:
            return made[name]
        kind, rest = name[0], name[1:]
        if kind == "mirror":
            cols = pl.ds(rest[0] * WIDE, WIDE)
            src, dst = stored.at[:, cols], mirrored.at[:, cols]
        elif kind == "meta":
            i = rest[0] * SIDE + rest[1]
            src, dst = notes.at[i], heard.at[row]
        elif kind == "route":
            i = rest[0] * SIDE + rest[1]
            src, dst = outgoing.at[i], slots.at[col, row]
        elif kind in WEIGHTS:
            h, s = rest[0], rest[-1]
            if kind == "line":
                where = chunk(h, 0, 0, 0)
            elif kind == "linepass":
                where = chunk(h, -s, 0, s)
            elif kind == "plane":
                where = chunk(h, rest[1], 0, 0)
            else:
                where = chunk(h, rest[1], -s, s)
            src = dst = weights.at[where]
        else:
            g = rest[0]
            if kind in ("own",):
                src = held(0, g, 0)
            elif kind == "ring":
                src = held(0, g, 0)
            elif kind == "ringpass":
                src = held(-rest[1], g, rest[1])
            elif kind == "share":
                src = held(-rest[1], g, 0)
            else:
                src = held(2, g, rest[1])
            dst = src
        i = index[name]
        made[name] = pltpu.make_async_remote_copy(
            src_ref=src, dst_ref=dst, send_sem=sent.at[i], recv_sem=came.at[i],
            device_id=device(copies[name][0]), device_id_type=pl.DeviceIdType.MESH,
        )
        return made[name]

    def halves(value):
        top = value.astype(jnp.bfloat16)
        return top, (value - top.astype(jnp.float32)).astype(jnp.bfloat16)

    earlier = (
        lax.broadcasted_iota(jnp.int32, (CAP, CAP), 0) < lax.broadcasted_iota(jnp.int32, (CAP, CAP), 1)
    ).astype(jnp.float32).astype(jnp.bfloat16)
    count = jnp.zeros((16, 1), jnp.float32)
    for b in range(ROWS // CAP):
        names = own[:, b * CAP : (b + 1) * CAP]
        hit = lax.broadcasted_iota(jnp.int32, (16, CAP), 0) == names
        one = jnp.where(hit, 1.0, 0.0)
        running = jnp.dot(one.astype(jnp.bfloat16), earlier, preferred_element_type=jnp.float32) + count
        places[:, b * CAP : (b + 1) * CAP] = jnp.where(hit, running, -1.0)
        count = count + jnp.sum(one, axis=1, keepdims=True)

    load.wait()
    top_amp[...], rest_amp[...] = halves(outgoing[0 : ROWS // CAP].reshape(ROWS, PART))
    gap_top, gap_rest = halves(gap[...])
    gap_rest = gap[...] - gap_top.astype(jnp.float32)
    gap_mid, gap_end = halves(gap_rest)
    pieces = [
        gap_top.astype(jnp.float32),
        gap_mid.astype(jnp.float32),
        gap_end.astype(jnp.float32),
        (irrep[...] + 1).astype(jnp.float32),
    ]
    tags = jnp.concatenate(pieces + [jnp.zeros((12, ROWS), jnp.float32)], axis=0).astype(jnp.bfloat16)

    pl.semaphore_wait(barrier, len(partners))
    started = []

    def start(name):
        copy(name).start()
        started.append(name)

    for h in range(QUARTERS):
        start(("mirror", h))

    def slotted(owner):
        place = places[pl.ds(owner, 1), :]
        pick = lax.broadcasted_iota(jnp.int32, (CAP, ROWS), 0).astype(jnp.float32) == place
        pick = jnp.where(pick, 1.0, 0.0).astype(jnp.bfloat16)
        block = jnp.dot(pick, top_amp[...], preferred_element_type=jnp.float32)
        block += jnp.dot(pick, rest_amp[...], preferred_element_type=jnp.float32)
        note = lax.dot_general(tags, pick, (((1,), (1,)), ((), ())), preferred_element_type=jnp.float32)
        return block, note[0:8]

    def slot_group(g):
        for dx in (0, 1, 3, 2):
            there = ((y - STEPS[g] + SIDE) % SIDE) * SIDE + (x - dx + SIDE) % SIDE
            block, note = slotted(there)
            i = g * SIDE + dx
            if i == 0:
                slots[col, row] = block
                heard[row] = note
            else:
                outgoing[i] = block
                notes[i] = note
                start(("route", g, dx))
                start(("meta", g, dx))

    parity = (1 - 2 * flags[col]).astype(jnp.float32)

    def split(where, n):
        rows, cols = where
        first = rows.start

        def body(i, carry):
            at = pl.ds(pl.multiple_of(first + i * 32, 32), 32)
            high[at, cols], low[at, cols] = halves(weights[at, cols])
            return carry

        lax.fori_loop(0, n // 32, body, 0)

    pairs, begun = [], {}

    def write(g, half):
        n = pairs.index((g, half)) % ROOM
        return pltpu.make_async_copy(
            sums.at[n],
            cycle.at[pl.ds(pl.multiple_of(group(STEPS[g]) * CAP, GROUP), GROUP), pl.ds(half * SET, SET)],
            done.at[n],
        )

    def multiply(g, half, dz):
        if (g, half) not in pairs:
            pairs.append((g, half))
            if len(pairs) > ROOM:
                write(*pairs[-1 - ROOM]).wait()
        into = sums.at[pairs.index((g, half)) % ROOM]
        c = (z + dz + SIDE) % SIDE
        both = [
            slots[c * CORES + half, pl.ds(group(STEPS[g]), SIDE)].reshape(GROUP, PART) for half in range(CORES)
        ]
        top, rest = halves(jnp.concatenate(both, axis=1))
        at = pl.ds(pl.multiple_of(c * (CORES * PART), CORES * PART), CORES * PART)
        for n in range(0, SET, 256):
            cols = pl.ds(half * SET + n, 256)
            w = high[at, cols]
            add = jnp.dot(top, w, preferred_element_type=jnp.float32)
            add += jnp.dot(rest, w, preferred_element_type=jnp.float32)
            add += jnp.dot(top, low[at, cols], preferred_element_type=jnp.float32)
            if (g, half) in begun:
                into[:, n : n + 256] += add
            else:
                into[:, n : n + 256] = add
        begun[g, half] = begun.get((g, half), 0) + 1
        if begun[g, half] == SIDE:
            write(g, half).start()

    seen = set()

    def follow(name):
        seen.add(name)
        for other, (_, after, _) in copies.items():
            if other not in started and name in after and all(n in seen for n in after):
                start(other)

    for act, name in schedule(copies):
        if act == "unit":
            multiply(*name)
            continue
        if act == "slot":
            slot_group(name)
            follow((act, name))
            continue
        copy(name).wait_recv()
        kind = name[0]
        if kind == "mirror":
            cols = pl.ds(name[1] * WIDE, WIDE)
            mine = chunk(name[1], 0, 0, 0)
            weights[mine] = stored[:, cols] + parity * mirrored[:, cols]
        follow(name)
        if kind == "mirror":
            split(mine, CHUNK)
        if kind in WEIGHTS:
            h, s = name[1], name[-1]
            if kind == "line":
                split(chunk(h, -s, 0, 0), CHUNK)
            elif kind == "linepass":
                split(chunk(h, -2 * s, 0, s), CHUNK // 2)
            elif kind == "plane":
                split(chunk(h, name[2], -s, 0), CHUNK)
            else:
                split(chunk(h, name[2], -2 * s, s), CHUNK // 2)

    for n in copies:
        if n[0] == "meta":
            copy(n).wait_recv()
    for i in range(16):
        meta[i] = heard[i]
    for n in copies:
        copy(n).wait_send()
    for pair in pairs[-ROOM:]:
        write(*pair).wait()


def exchange(amp, own, gap, irrep, stored, flags):
    n = len(plan())
    vmem = pl.BlockSpec(memory_space=pltpu.VMEM)
    return pl.pallas_call(
        kernel,
        out_shape=(
            jax.ShapeDtypeStruct((16 * CAP, LANES), jnp.float32),
            jax.ShapeDtypeStruct((16, 8, CAP), jnp.float32),
        ),
        in_specs=[pl.BlockSpec(memory_space=pl.ANY)] + [vmem] * 4 + [pl.BlockSpec(memory_space=pltpu.SMEM)],
        out_specs=(pl.BlockSpec(memory_space=pl.ANY), vmem),
        scratch_shapes=[
            pltpu.VMEM((SIDE * CORES, 16, CAP, PART), jnp.float32),
            pltpu.VMEM((DEPTH, LANES), jnp.float32),
            pltpu.VMEM((DEPTH, LANES), jnp.bfloat16),
            pltpu.VMEM((DEPTH, LANES), jnp.bfloat16),
            pltpu.VMEM((ROWS, PART), jnp.bfloat16),
            pltpu.VMEM((ROWS, PART), jnp.bfloat16),
            pltpu.VMEM((ROOM, GROUP, SET), jnp.float32),
            pltpu.VMEM((16, CAP, PART), jnp.float32),
            pltpu.VMEM((CHUNK, LANES), jnp.float32),
            pltpu.VMEM((16, ROWS), jnp.float32),
            pltpu.VMEM((16, 8, CAP), jnp.float32),
            pltpu.VMEM((16, 8, CAP), jnp.float32),
            pltpu.SemaphoreType.DMA((n,)),
            pltpu.SemaphoreType.DMA((n,)),
            pltpu.SemaphoreType.DMA((ROOM + 1,)),
        ],
        compiler_params=pltpu.CompilerParams(
            collective_id=0, has_side_effects=True, vmem_limit_bytes=60 * 2**20
        ),
        name="exchange",
    )(amp, own, gap, irrep, stored, flags)


def per_device(amplitudes, row_gap, row_irrep, owners, stored, col_gap, col_irrep, mirror_flags):
    line = (1, ROWS)
    cycle, meta = exchange(
        amplitudes.reshape(ROWS // CAP, CAP, PART), owners.reshape(line), row_gap.reshape(line), row_irrep.reshape(line), stored, mirror_flags
    )
    gap = (meta[:, 0] + meta[:, 1] + meta[:, 2]).reshape(-1, 1)
    irrep = (meta[:, 3] - 1.0).reshape(-1, 1)
    same = irrep == col_irrep.astype(jnp.float32)[None, :]
    return jnp.where(same, cycle / (gap + col_gap[None, :]), 0.0)


def solution(mesh):
    placed = (
        P("row", "col"),
        P("row"),
        P("row"),
        P("row", None),
        P("row", "col"),
        P("col"),
        P("col"),
        P(),
    )
    return jax.shard_map(
        per_device, mesh=mesh, in_specs=placed, out_specs=P("row", "col"), check_vma=False
    )
```

time: 196 us -> 168 us (0.86); the launches traced: 193 us -> 167 us
  Pallas kernels: 185 us -> 159 us
    pallas_call x1, Pallas kernels: 185 us -> 159 us  [exchange(): pl.pallas_call(kernel, out_shape=(jax.ShapeDtypeStruct((16 * CAP, LANES),...]
where the time goes in v3:
time: 168 us; the launch traced here: 167 us
  Pallas kernels  159 us (95%)
  other arithmetic  8.06 us (5%)
    pallas_call x1, Pallas kernels, exchange(): pl.pallas_call(kernel, out_shape=(jax.ShapeDtypeStruct((16 * CAP, LANES),...  159 us
    select_n x1, other arithmetic, per_device(): return jnp.where(same, cycle / (gap + col_gap[None, :]), 0.0)  6.36 us

profile of v3, /device:TPU:0, one launch (start us, length us, event | category | flops | bytes accessed | tf_op | source)
XLA Modules:
  0.0 166.9 jit_solution(1883244818947155396)
XLA Ops:
  0.0 0.7 convert_element_type.3
  0.7 158.9 %exchange.1 = (f32[2048,1024]{1,0:T(8,128)}, f32[16,8,128]{2,1,0:T(8,128)}) custom-call(f32[8,128,384]{2,1,0:T(8,128)} %bitcast.6, s32[1,1024]{1,0:T(1,128)} %bitcast.9, f32[1,1024]{1,0:T(1,128)} %bitcast.10, s32[1,1024]{1,0:T(1,128)} %bitcast.11, f32[192,1024]{1,0:T(8,128)} %stored.1, s32[8]{0:T(128)} %flags.1), custom_call_target="tpu_custom_call" | custom-call | tf_op jit(solution)/shard_map/exchange/pallas_call | solution.py:393
  159.5 1.0 slice_add_fusion.1
  160.6 6.4 %divide_select_fusion = f32[2048,1024]{1,0:T(8,128)} fusion(f32[2048,1024]{1,0:T(8,128)} %get-tuple-element.8, f32[1024]{0:T(1024)} %param.13, f32[2048]{0:T(1024)S(1)} %bitcast.8, f32[1024]{0:T(1024)S(1)} %convert_element_type.3, f32[2048]{0:T(1024)S(1)} %bitcast.7), kind=kLoop, calls=%fused_computation | loop fusion | flops 8388608 | bytes 16801792 | tf_op jit(solution)/shard_map/jit(_where)/select_n | solution.py:433
